TPU v7x, 256 devices: a whole 4x4x8 slice. The times are simulated.
256 devices in a mesh: layer: 2 (over z_lo), row: 8 (over y, core), col: 16 (over z_hi, x).
Axes of the slice: x: 4, y: 4, z: 8 (z_hi: 4, z_lo: 2; z = z_hi * 2 + z_lo), core: 2. Of those that a mesh axis runs over, the one named last changes fastest.
Arguments:
- matrix: float32 [16384, 16384], P('row', 'col'), may hold values from -1.5 to 1.5, as said below
Outputs:
- square_panel: float32 [16384, 512], P('row', 'layer')
- new_panel: float32 [16384, 512], P('row', 'layer')
Inputs may be any that keep to these rules, and one draw needn't show every extreme that they name: `matrix`: entries off the diagonal are of order 0.5 / sqrt(16384); the diagonal's magnitudes lie between 0.6 and 1 with either sign.
All inputs are finite; a program needn't handle non-finite values.
Results may differ from a plain program's by a relative error of at most 0.000076.
Values sent between devices are 32-bit elements; how exact they have to be, the bound alone decides.
A program may use at most 128 MiB of HBM per device.

v0:
```python
import jax
import jax.numpy as jnp
from jax import lax
from jax.sharding import PartitionSpec as P

PW = 512


def from_root(shard, axis, root):
    mine = lax.axis_index(axis) == root
    return lax.psum(jnp.where(mine, shard, jnp.zeros_like(shard)), axis)


def matmul_high(left_side, right_side):
    return jnp.dot(
        left_side, right_side, precision=lax.Precision.HIGHEST, preferred_element_type=jnp.float32
    )


def body(matrix):
    block_cols = matrix.shape[1]
    layers = lax.axis_size("layer")
    col_ratio = lax.axis_size("col") // lax.axis_size("row")
    col_index = lax.axis_index("col")
    layer_index = lax.axis_index("layer")
    half_width = PW // layers
    root_row = col_index // col_ratio
    offset = col_index % col_ratio * block_cols
    panel_full = from_root(matrix[:, :PW], "col", 0)
    own_cols = lax.dynamic_slice_in_dim(panel_full, layer_index * half_width, half_width, 1)
    depth_rows = block_cols // layers
    first_row = offset + layer_index * depth_rows
    panel_slab = from_root(
        lax.dynamic_slice_in_dim(panel_full, first_row, depth_rows, 0), "row", root_row
    )
    local_cols = lax.dynamic_slice_in_dim(matrix, layer_index * depth_rows, depth_rows, 1)
    square_full = lax.psum(matmul_high(local_cols, panel_slab), ("layer", "col"))
    square_slab = from_root(
        lax.dynamic_slice_in_dim(square_full, first_row, depth_rows, 0), "row", root_row
    )
    update = lax.psum_scatter(
        matmul_high(local_cols, square_slab), "layer", scatter_dimension=1, tiled=True
    )
    update = lax.psum(update, "col")
    square = lax.dynamic_slice_in_dim(square_full, layer_index * half_width, half_width, 1)
    new_panel = (3.0 * own_cols - update) * 0.5
    return (square, new_panel)


def solution(mesh):
    placed = (P("row", "col"),)
    return jax.shard_map(
        body,
        mesh=mesh,
        in_specs=placed,
        out_specs=(P("row", "layer"), P("row", "layer")),
        check_vma=False,
    )
```

profile of v0, /device:TPU:16, one launch (start us, length us, event | category | flops | bytes accessed | tf_op | source)
XLA Modules:
  0.0 809.4 jit_solution(460881230599396828)
XLA Ops:
  7.2 0.0 all-reduce.6.cloned.1.call-start
  7.2 4.6 slice_select_fusion
  11.9 0.0 all-reduce.6.cloned.1.call-update
  11.9 0.0 all-reduce.8.cloned.1.call-start
  12.0 224.7 %all-reduce.6.cloned.1.call-done = f32[2048,512]{1,0:T(8,128)} async-done(((f32[2048,512]{1,0:T(8,128)}), f32[2048,512]{1,0:T(8,128)}) %all-reduce.6.cloned.1.call-update) | async-done | bytes 4194320 | tf_op jit(solution)/shard_map/psum | solution.py:11
  236.6 2.3 dynamic-slice_select_fusion.1
  238.9 0.0 all-reduce.8.cloned.1.call-update
  239.0 0.0 all-reduce.10.cloned.1.call-start
  239.0 61.4 %all-reduce.8.cloned.1.call-done = f32[512,512]{1,0:T(8,128)} async-done(((f32[512,512]{1,0:T(8,128)}), f32[512,512]{1,0:T(8,128)}) %all-reduce.8.cloned.1.call-update) | async-done | bytes 1048592 | tf_op jit(solution)/shard_map/psum | solution.py:11
  300.4 10.1 %fusion.2 = f32[2048,512]{1,0:T(8,128)} fusion(f32[512,512]{1,0:T(8,128)} %all-reduce.8.cloned.1.call-done, f32[2048,1024]{1,0:T(8,128)} %param.1, s32[]{:T(128)S(6)} %select_n.42), kind=kOutput, calls=%fused_computation.3 | convolution fusion | flops 6442450944 | bytes 9437188 | tf_op jit(solution)/shard_map/dot_general | solution.py:15
  310.5 0.0 all-reduce.10.cloned.1.call-update
  310.5 0.0 all-reduce.12.cloned.1.call-start
  310.6 167.7 %all-reduce.10.cloned.1.call-done = f32[2048,512]{1,0:T(8,128)} async-done(((f32[2048,512]{1,0:T(8,128)}), f32[2048,512]{1,0:T(8,128)}) %all-reduce.10.cloned.1.call-update) | async-done | bytes 4194320 | tf_op jit(solution)/shard_map/psum | solution.py:37
  478.2 2.3 dynamic-slice_select_fusion
  480.5 0.0 all-reduce.12.cloned.1.call-update
  480.6 0.0 reduce-scatter.2.cloned.1.call-start
  480.6 61.5 %all-reduce.12.cloned.1.call-done = f32[512,512]{1,0:T(8,128)} async-done(((f32[512,512]{1,0:T(8,128)}), f32[512,512]{1,0:T(8,128)}) %all-reduce.12.cloned.1.call-update) | async-done | bytes 1048592 | tf_op jit(solution)/shard_map/psum | solution.py:11
  542.1 10.1 %fusion = f32[2048,512]{1,0:T(8,128)} fusion(f32[512,512]{1,0:T(8,128)} %all-reduce.12.cloned.1.call-done, f32[2048,1024]{1,0:T(8,128)} %param.1, s32[]{:T(128)S(6)} %select_n.42), kind=kOutput, calls=%fused_computation.1 | convolution fusion | flops 6442450944 | bytes 9437188 | tf_op jit(solution)/shard_map/dot_general | solution.py:15
  552.2 0.0 reduce-scatter.2.cloned.1.call-update
  552.2 0.0 all-reduce.14.cloned.1.call-start
  552.2 62.9 %reduce-scatter.2.cloned.1.call-done = f32[2048,256]{1,0:T(8,128)} async-done(((f32[2048,512]{1,0:T(8,128)}), f32[2048,256]{1,0:T(8,128)}) %reduce-scatter.2.cloned.1.call-update) | async-done | bytes 2097168 | tf_op jit(solution)/shard_map/reduce_scatter | solution.py:41
  615.2 0.0 all-reduce.14.cloned.1.call-update
  615.2 3.0 constant_dynamic-slice_fusion
  618.3 180.5 %all-reduce.14.cloned.1.call-done = f32[2048,256]{1,0:T(8,128)} async-done(((f32[2048,256]{1,0:T(8,128)}), f32[2048,256]{1,0:T(8,128)}) %all-reduce.14.cloned.1.call-update) | async-done | bytes 2097168 | tf_op jit(solution)/shard_map/psum | solution.py:44
  798.7 3.8 subtract_multiply_fusion
Async XLA Ops:
  7.2 229.5 %all-reduce.6.cloned.1.call-start = ((), (), s32[]{:S(2)}) async-start(), calls=%async_computation.1 | async-start | bytes 8388608 | tf_op jit(solution)/shard_map/psum | solution.py:11
  11.9 288.5 %all-reduce.8.cloned.1.call-start = ((), (), s32[]{:S(2)}) async-start(), calls=%async_computation.2 | async-start | bytes 2097152 | tf_op jit(solution)/shard_map/psum | solution.py:11
  239.0 239.3 %all-reduce.10.cloned.1.call-start = ((), (), s32[]{:S(2)}) async-start(), calls=%async_computation.3 | async-start | bytes 8388608 | tf_op jit(solution)/shard_map/psum | solution.py:37
  310.5 231.6 %all-reduce.12.cloned.1.call-start = ((), (), s32[]{:S(2)}) async-start(), calls=%async_computation.4 | async-start | bytes 2097152 | tf_op jit(solution)/shard_map/psum | solution.py:11
  480.6 134.6 %reduce-scatter.2.cloned.1.call-start = ((), (), s32[]{:S(2)}) async-start(), calls=%async_computation.5 | async-start | bytes 6291456 | tf_op jit(solution)/shard_map/reduce_scatter | solution.py:41
  552.2 246.5 %all-reduce.14.cloned.1.call-start = ((), (), s32[]{:S(2)}) async-start(), calls=%async_computation.6 | async-start | bytes 4194304 | tf_op jit(solution)/shard_map/psum | solution.py:44
Sparse Core Ops, SparseCore 0:
  12.0 224.5 all-reduce.5
  239.6 60.7 all-reduce.7
  310.6 167.5 all-reduce.9
  481.0 61.0 all-reduce.11
  552.3 62.8 reduce-scatter.1
  617.7 180.9 all-reduce.13
where the time goes:
time: 810 us; the launch traced here: 809 us
  waiting for transfers between devices  759 us (94%)
  matrix products  20.1 us (2%)
  between operations  14.2 us (2%)
  other arithmetic  13 us (2%)
    psum x3, waiting for transfers between devices, from_root(): return lax.psum(jnp.where(mine, shard, jnp.zeros_like(shard)), axis)  348 us
    psum x1, waiting for transfers between devices, body(): update = lax.psum(update, 'col')  180 us
    psum x1, waiting for transfers between devices, body(): lax.psum(matmul_high(local_cols, panel_slab), ('layer', 'col'))  168 us
    reduce_scatter x1, waiting for transfers between devices, body(): lax.psum_scatter(matmul_high(local_cols, square_slab), 'layer', scatter_d...  62.9 us
    dot_general x2, matrix products, matmul_high(): jnp.dot(left_side, right_side, precision=lax.Precision.HIGHEST, preferred...  20.1 us
  transfers between devices with their start and end apart: 6, of which 6 were waited for; matrix products, arithmetic and copies ran while one was open for 0% of the time, Pallas kernels for 0%

commit v1 on v0

v1 whole, which is shorter than its diff:
```python
import functools

import jax
import jax.numpy as jnp
from jax import lax
from jax.experimental import pallas as pl
from jax.experimental.pallas import tpu as pltpu
from jax.sharding import PartitionSpec as P

MESH = pl.DeviceIdType.MESH
F32 = jnp.float32
BF16 = jnp.bfloat16

CHUNKS = 2
W = 128
LAG = 2
ROWS = 2048
DEPTH = 1024
SLICE = 512
SUB = 128
TILE = 256
NSEM = 160


class Sems:
    def __init__(self, send, recv):
        self.send, self.recv, self.n, self.pending = send, recv, 0, []

    def new(self):
        self.n += 1
        assert self.n <= NSEM
        return self.n - 1

    def copy(self, src, dst, slot, device):
        return pltpu.make_async_remote_copy(
            src_ref=src,
            dst_ref=dst,
            send_sem=self.send.at[slot],
            recv_sem=self.recv.at[slot],
            device_id=device,
            device_id_type=MESH,
        )


def kernel(
    x_hbm, s_hbm, n_hbm,
    xf, xh, xl, pb, pc, sc, hl, part, rx1, rx2, rz1, rz2, full,
    send_sem, recv_sem, load_sem, panel_sem, out_sem,
):
    layer = lax.axis_index("layer")
    row = lax.axis_index("row")
    col = lax.axis_index("col")
    y, q = lax.div(row, 2), lax.rem(row, 2)
    zh, x = lax.div(col, 4), lax.rem(col, 4)
    owner_core = lax.div(x, 2)
    half = lax.rem(x, 2)
    sems = Sems(send_sem, recv_sem)
    drains = []

    def m8(value, n):
        return pl.ds(pl.multiple_of(value, 64), n)

    def at_x(d):
        return {"col": zh * 4 + lax.rem(x + d, 4)}

    def at_z(d):
        return {"col": lax.rem(zh + d, 4) * 4 + x}

    def at_y(d):
        return {"row": lax.rem(y + d, 4) * 2 + q}

    partner = {"row": y * 2 + 1 - q}
    fetches = q == owner_core
    has_panel = col == 0
    origin = jnp.logical_and(jnp.logical_and(y == 0, q == 0), has_panel)

    loads = [
        pltpu.make_async_copy(
            x_hbm.at[pl.ds(i * TILE, TILE), :], xf.at[pl.ds(i * TILE, TILE), :], load_sem.at[i]
        )
        for i in range(ROWS // TILE)
    ]
    panel_loads = [
        pltpu.make_async_copy(
            x_hbm.at[:, pl.ds(pl.multiple_of(layer * (CHUNKS * W) + k * W, W), W)],
            pb.at[k],
            panel_sem.at[k],
        )
        for k in range(CHUNKS)
    ]

    @pl.when(has_panel)
    def _():
        for load in panel_loads:
            load.start()

    for load in loads:
        load.start()

    barrier = pltpu.get_barrier_semaphore()
    for device in (at_x(1), at_x(3), at_z(1), at_z(3), at_y(1), at_y(2), at_y(3), partner):
        pl.semaphore_signal(barrier, inc=1, device_id=device, device_id_type=MESH)

    @pl.when(jnp.logical_and(fetches, jnp.logical_not(origin)))
    def _():
        pl.semaphore_signal(
            barrier, inc=1, device_id={"row": zh * 2 + q, "col": 0}, device_id_type=MESH
        )

    @pl.when(has_panel)
    def _():
        pl.semaphore_wait(barrier, 16 - jnp.where(row == 0, 1, 0))

    @pl.when(jnp.logical_not(has_panel))
    def _():
        pl.semaphore_wait(barrier, 8)

    def owned(d):
        u = lax.rem(x + d - 2 * q + 4, 4)
        return (2 * lax.rem(lax.div(u + 1, 2), 2) + lax.div(u, 2)) * SLICE

    x_rows = [owned(d) for d in range(4)]

    def z_rows(d):
        return x_rows[0] + lax.rem(zh + d, 4) * SUB

    def reduce_start(buf, r1, rows, size, at):
        h = size // 2
        a = sems.copy(buf.at[m8(rows[2], h)], r1.at[0], sems.new(), at(1))
        b = sems.copy(buf.at[m8(rows[2] + h, h)], r1.at[1], sems.new(), at(3))
        a.start()
        b.start()
        drains.extend([a, b])
        return a, b

    def reduce_own(buf, r2, rows, size, at):
        h = size // 2
        a = sems.copy(buf.at[m8(rows[1] + h, h)], r2.at[0, pl.ds(h, h)], sems.new(), at(1))
        b = sems.copy(buf.at[m8(rows[3], h)], r2.at[1, pl.ds(0, h)], sems.new(), at(3))
        a.start()
        b.start()
        drains.extend([a, b])
        return a, b

    def reduce_middle(buf, r1, r2, rows, size, at, first):
        h = size // 2
        first[0].wait_recv()
        buf[m8(rows[1], h)] += r1[0]
        a = sems.copy(buf.at[m8(rows[1], h)], r2.at[0, pl.ds(0, h)], sems.new(), at(1))
        a.start()
        first[1].wait_recv()
        buf[m8(rows[3] + h, h)] += r1[1]
        b = sems.copy(buf.at[m8(rows[3] + h, h)], r2.at[1, pl.ds(h, h)], sems.new(), at(3))
        b.start()
        drains.extend([a, b])
        return a, b

    def gather_start(buf, rows, size, at):
        a = sems.copy(buf.at[m8(rows[0], size)], buf.at[m8(rows[0], size)], sems.new(), at(1))
        b = sems.copy(buf.at[m8(rows[0], size)], buf.at[m8(rows[0], size)], sems.new(), at(3))
        a.start()
        b.start()
        drains.extend([a, b])
        return a, b

    def gather_middle(buf, rows, size, at, first):
        h = size // 2
        first[0].wait_recv()
        a = sems.copy(buf.at[m8(rows[3], h)], buf.at[m8(rows[3], h)], sems.new(), at(1))
        a.start()
        first[1].wait_recv()
        b = sems.copy(buf.at[m8(rows[1] + h, h)], buf.at[m8(rows[1] + h, h)], sems.new(), at(3))
        b.start()
        drains.extend([a, b])
        return a, b

    def split_rhs(src, k):
        def tile(i, carry):
            rows = pl.ds(pl.multiple_of(i * TILE, TILE), TILE)
            value = src[rows, :]
            hi = value.astype(BF16)
            hl[k, rows, pl.ds(0, W)] = hi
            hl[k, rows, pl.ds(W, W)] = (value - hi.astype(F32)).astype(BF16)
            return carry

        lax.fori_loop(0, DEPTH // TILE, tile, 0)

    def product(buf, k, first_row):
        def tile(i, carry):
            rows = pl.ds(pl.multiple_of(first_row + i * TILE, TILE), TILE)
            both = jnp.dot(xh[rows, :], hl[k], preferred_element_type=F32)
            low = jnp.dot(xl[rows, :], hl[k, :, pl.ds(0, W)], preferred_element_type=F32)
            buf[rows, :] = both[:, :W] + (both[:, W:] + low)
            return carry

        lax.fori_loop(0, SLICE // TILE, tile, 0)

    def minus_panel(buf, k, first_row):
        @pl.when(has_panel)
        def _():
            rows = m8(first_row, SLICE)
            buf[rows, :] -= 3.0 * pb[k, rows, :]

    def split_block():
        for i, load in enumerate(loads):
            load.wait()

        def tile(i, carry):
            rows = pl.ds(pl.multiple_of(i * 64, 64), 64)
            value = xf[rows, :]
            hi = value.astype(BF16)
            xh[rows, :] = hi
            xl[rows, :] = (value - hi.astype(F32)).astype(BF16)
            return carry

        lax.fori_loop(0, ROWS // 64, tile, 0)

    def chain(k):
        steps = []
        state = {}

        quarter = DEPTH // 4
        spread = [sems.new() for _ in range(1)]
        sent_panel = []

        def panel_send():
            @pl.when(has_panel)
            def _():
                panel_loads[k].wait()

            for h in range(2):
                for j in range(4):
                    slot = sems.new()
                    src = pb.at[k, pl.ds(h * DEPTH + j * quarter, quarter)]
                    dst = pc.at[k, pl.ds(j * quarter, quarter)]
                    copy = pltpu.make_async_remote_copy(
                        src_ref=src,
                        dst_ref=dst,
                        send_sem=send_sem.at[slot],
                        recv_sem=recv_sem.at[spread[0]],
                        device_id={"row": 2 * j + q, "col": y * 4 + 2 * q + h},
                        device_id_type=MESH,
                    )
                    if h == 0 and j == 0:

                        @pl.when(origin)
                        def _():
                            pc[k, pl.ds(0, quarter)] = pb[k, pl.ds(0, quarter)]

                        @pl.when(jnp.logical_and(has_panel, row != 0))
                        def _(copy=copy):
                            copy.start()
                    else:

                        @pl.when(has_panel)
                        def _(copy=copy):
                            copy.start()

                    sent_panel.append(copy)

            state["panel_sent"] = sent_panel

        ring = [sems.new() for _ in range(4)]
        share = [sems.new() for _ in range(4)]

        def mine(d):
            return m8(lax.rem(y + 4 - d, 4) * quarter, quarter)

        def ring_copy(d):
            return sems.copy(pc.at[k, mine(0)], pc.at[k, mine(0)], ring[d], at_y(d))

        def share_copy(d):
            return sems.copy(pc.at[k, mine(d)], pc.at[k, mine(d)], share[d], partner)

        def panel_ring():
            @pl.when(fetches)
            def _():
                @pl.when(jnp.logical_not(origin))
                def _():
                    pltpu.make_async_remote_copy(
                        src_ref=pc.at[k, mine(0)],
                        dst_ref=pc.at[k, mine(0)],
                        send_sem=send_sem.at[spread[0]],
                        recv_sem=recv_sem.at[spread[0]],
                        device_id=partner,
                        device_id_type=MESH,
                    ).wait_recv()

                for d in (1, 3, 2):
                    ring_copy(d).start()
                share_copy(0).start()

        def panel_share():
            @pl.when(fetches)
            def _():
                for d in (1, 3, 2):
                    ring_copy(d).wait_recv()
                    share_copy(d).start()

            @pl.when(jnp.logical_not(fetches))
            def _():
                for d in range(4):
                    share_copy(d).wait_recv()

        def panel_drain():
            for i, copy in enumerate(sent_panel):
                cond = jnp.logical_and(has_panel, row != 0) if i == 0 else has_panel

                @pl.when(cond)
                def _(copy=copy):
                    copy.wait_send()

            @pl.when(fetches)
            def _():
                for d in range(4):
                    if d:
                        ring_copy(d).wait_send()
                    share_copy(d).wait_send()

        def multiply(phase):
            buf = part.at[phase, k]

            def run(first_row):
                product(buf, k, first_row)
                if phase == 1:
                    minus_panel(buf, k, first_row)

            def step():
                if phase == 0 and k == 0:
                    split_block()
                split_rhs((pc if phase == 0 else sc).at[k], k)
                run(x_rows[2])
                state[phase, "x1"] = reduce_start(buf, rx1.at[phase, k], x_rows, SLICE, at_x)
                run(x_rows[1])
                run(x_rows[3])
                state[phase, "x2"] = reduce_own(buf, rx2.at[phase, k], x_rows, SLICE, at_x)
                run(x_rows[0])

            return step

        def reduce_steps(phase):
            buf = part.at[phase, k]
            out = full.at[phase, k]
            zr = [z_rows(d) for d in range(4)]

            def x_middle():
                state[phase, "x3"] = reduce_middle(
                    buf, rx1.at[phase, k], rx2.at[phase, k], x_rows, SLICE, at_x, state[phase, "x1"]
                )

            def x_end():
                for copy in state[phase, "x2"] + state[phase, "x3"]:
                    copy.wait_recv()
                rows = m8(x_rows[0], SLICE)
                buf[rows] += rx2[phase, k, 0] + rx2[phase, k, 1]
                state[phase, "z1"] = reduce_start(buf, rz1.at[phase, k], zr, SUB, at_z)
                state[phase, "z2"] = reduce_own(buf, rz2.at[phase, k], zr, SUB, at_z)

            def z_middle():
                state[phase, "z3"] = reduce_middle(
                    buf, rz1.at[phase, k], rz2.at[phase, k], zr, SUB, at_z, state[phase, "z1"]
                )

            def z_end():
                for copy in state[phase, "z2"] + state[phase, "z3"]:
                    copy.wait_recv()
                rows = m8(zr[0], SUB)
                total = buf[rows] + (rz2[phase, k, 0] + rz2[phase, k, 1])
                out[rows] = total if phase == 0 else total * -0.5
                state[phase, "g1"] = gather_start(out, zr, SUB, at_z)

            def gz_middle():
                state[phase, "g2"] = gather_middle(out, zr, SUB, at_z, state[phase, "g1"])

            return [x_middle, x_end, z_middle, z_end, gz_middle]

        def gather_x(phase):
            out = full.at[phase, k]

            def start():
                for copy in state[phase, "g2"]:
                    copy.wait_recv()
                state[phase, "g3"] = gather_start(out, x_rows, SLICE, at_x)

            def middle():
                state[phase, "g4"] = gather_middle(out, x_rows, SLICE, at_x, state[phase, "g3"])

            def end():
                for copy in state[phase, "g4"]:
                    copy.wait_recv()
                store = pltpu.make_async_copy(
                    out,
                    (s_hbm if phase == 0 else n_hbm).at[:, pl.ds(k * W, W)],
                    out_sem.at[phase, k],
                )
                store.start()
                state[phase, "store"] = store

            return start, middle, end

        turn = lax.rem(y - zh + 4, 4)
        root = jnp.logical_and(fetches, turn == 0)
        y1 = jnp.logical_and(fetches, turn == 1)
        y2 = jnp.logical_and(fetches, turn == 2)
        y3 = jnp.logical_and(fetches, turn == 3)
        slab = [m8(half * DEPTH + i * SLICE, SLICE) for i in range(2)]
        fwd = [[sems.new() for _ in range(2)] for _ in range(4)]

        def from_root(i, d):
            return sems.copy(full.at[0, k, slab[i]], sc.at[k, pl.ds(i * SLICE, SLICE)], fwd[d][i], at_y(d))

        def onward(i, d):
            block = sc.at[k, pl.ds(i * SLICE, SLICE)]
            return sems.copy(block, block, fwd[2][i], at_y(d))

        def across(i):
            block = sc.at[k, pl.ds(i * SLICE, SLICE)]
            return sems.copy(block, block, fwd[0][i], partner)

        def send_slab(i):
            @pl.when(root)
            def _():
                from_root(i, 1).start()
                from_root(i, 3).start()
                sc[k, pl.ds(i * SLICE, SLICE)] = full[0, k, slab[i]]
                across(i).start()

        def pass_slab():
            @pl.when(y1)
            def _():
                from_root(0, 1).wait_recv()
                onward(0, 1).start()
                across(0).start()
                from_root(1, 1).wait_recv()
                across(1).start()

            @pl.when(y3)
            def _():
                from_root(0, 3).wait_recv()
                across(0).start()
                from_root(1, 3).wait_recv()
                onward(1, 3).start()
                across(1).start()

        def end_slab():
            @pl.when(y2)
            def _():
                onward(0, 1).wait_recv()
                across(0).start()
                onward(1, 3).wait_recv()
                across(1).start()

            @pl.when(jnp.logical_not(fetches))
            def _():
                across(0).wait_recv()
                across(1).wait_recv()

        def slab_drain():
            @pl.when(root)
            def _():
                for i in range(2):
                    from_root(i, 1).wait_send()
                    from_root(i, 3).wait_send()

            @pl.when(y1)
            def _():
                onward(0, 1).wait_send()

            @pl.when(y3)
            def _():
                onward(1, 3).wait_send()

            @pl.when(fetches)
            def _():
                across(0).wait_send()
                across(1).wait_send()

        s_start, s_middle, s_end = gather_x(0)
        u_start, u_middle, u_end = gather_x(1)

        def s_start_and_slab():
            s_start()
            send_slab(0)

        def s_middle_and_slab():
            s_middle()
            send_slab(1)

        def pass_on():
            pass_slab()

        def multiply_again():
            end_slab()
            multiply(1)()

        second = reduce_steps(1)

        def finish():
            s_end()

        steps += [panel_send, panel_ring, panel_share, multiply(0)]
        steps += reduce_steps(0)
        steps += [s_start_and_slab, s_middle_and_slab, pass_on, multiply_again]
        steps += [second[0], finish] + second[1:]
        steps += [u_start, u_middle, u_end]
        return steps, [panel_drain, slab_drain], state

    chains = [chain(k) for k in range(CHUNKS)]
    for t in range(len(chains[0][0]) + LAG * (CHUNKS - 1)):
        for k in range(CHUNKS):
            if 0 <= t - LAG * k < len(chains[k][0]):
                chains[k][0][t - LAG * k]()
    for copy in drains:
        copy.wait_send()
    for steps, ends, state in chains:
        for end in ends:
            end()
        for phase in range(2):
            state[phase, "store"].wait()


def solution(mesh):
    def body(matrix):
        return pl.pallas_call(
            kernel,
            out_shape=(
                jax.ShapeDtypeStruct((ROWS, CHUNKS * W), F32),
                jax.ShapeDtypeStruct((ROWS, CHUNKS * W), F32),
            ),
            in_specs=[pl.BlockSpec(memory_space=pl.ANY)],
            out_specs=(pl.BlockSpec(memory_space=pl.ANY), pl.BlockSpec(memory_space=pl.ANY)),
            scratch_shapes=[
                pltpu.VMEM((ROWS, DEPTH), F32),
                pltpu.VMEM((ROWS, DEPTH), BF16),
                pltpu.VMEM((ROWS, DEPTH), BF16),
                pltpu.VMEM((CHUNKS, ROWS, W), F32),
                pltpu.VMEM((CHUNKS, DEPTH, W), F32),
                pltpu.VMEM((CHUNKS, DEPTH, W), F32),
                pltpu.VMEM((CHUNKS, DEPTH, 2 * W), BF16),
                pltpu.VMEM((2, CHUNKS, ROWS, W), F32),
                pltpu.VMEM((2, CHUNKS, 2, SLICE // 2, W), F32),
                pltpu.VMEM((2, CHUNKS, 2, SLICE, W), F32),
                pltpu.VMEM((2, CHUNKS, 2, SUB // 2, W), F32),
                pltpu.VMEM((2, CHUNKS, 2, SUB, W), F32),
                pltpu.VMEM((2, CHUNKS, ROWS, W), F32),
                pltpu.SemaphoreType.DMA((NSEM,)),
                pltpu.SemaphoreType.DMA((NSEM,)),
                pltpu.SemaphoreType.DMA((ROWS // TILE,)),
                pltpu.SemaphoreType.DMA((CHUNKS,)),
                pltpu.SemaphoreType.DMA((2, CHUNKS)),
            ],
            compiler_params=pltpu.CompilerParams(
                collective_id=0, has_side_effects=True, vmem_limit_bytes=60 * 1024 * 1024
            ),
        )(matrix)

    return jax.shard_map(
        body,
        mesh=mesh,
        in_specs=(P("row", "col"),),
        out_specs=(P("row", "layer"), P("row", "layer")),
        check_vma=False,
    )
```

time: 810 us -> 218 us (0.27)
  waiting for transfers between devices: 759 us -> 0 us
  Pallas kernels: 0 us -> 211 us
  matrix products: 20.1 us -> 0 us
  between operations: 14.2 us -> 0.65 us
  other arithmetic: 13 us -> 0 us
    psum x5 -> x0, waiting for transfers between devices: 696 us -> none  [the longest x3 348 us: from_root(): return lax.psum(jnp.where(mine, shard, jnp.zeros_like(shard)), axis)]
    pallas_call x0 -> x1, Pallas kernels: none -> 211 us  [body(): pl.pallas_call(kernel, out_shape=(jax.ShapeDtypeStruct((ROWS, CHUNKS * W)...]
    reduce_scatter x1 -> x0, waiting for transfers between devices: 62.9 us -> none  [body(): lax.psum_scatter(matmul_high(local_cols, square_slab), 'layer', scatter_d...]
    dot_general x2 -> x0, matrix products: 20.1 us -> none  [matmul_high(): jnp.dot(left_side, right_side, precision=lax.Precision.HIGHEST, preferred...]
    select_n x3 -> x0, other arithmetic: 9.22 us -> none  [from_root(): return lax.psum(jnp.where(mine, shard, jnp.zeros_like(shard)), axis)]
  transfers between devices with their start and end apart: 6 -> 0, of which waited for: 6 -> 0; matrix products, arithmetic and copies ran while one was open for 0% -> 0% of each run, Pallas kernels for 0% -> 0%
where the time goes in v1:
time: 218 us; the launch traced here: 216 us
  Pallas kernels  211 us (97%)
  local copies, waits for them, and re-layouts  4.52 us (2%)
    pallas_call x1, Pallas kernels, body(): pl.pallas_call(kernel, out_shape=(jax.ShapeDtypeStruct((ROWS, CHUNKS * W)...  211 us
    unnamed x4, local copies, waits for them, and re-layouts  4.52 us

profile of v1, /device:TPU:16, one launch (start us, length us, event | category | flops | bytes accessed | tf_op | source)
XLA Modules:
  0.0 216.3 jit_solution(2577483251418199023)
XLA Ops:
  0.6 211.1 %shard_map.30 = (f32[2048,256]{1,0:T(8,128)}, f32[2048,256]{1,0:T(8,128)}) custom-call(f32[2048,1024]{1,0:T(8,128)} %x_hbm.1), custom_call_target="tpu_custom_call" | custom-call | tf_op jit(solution)/shard_map/pallas_call | solution.py:524
  211.8 0.0 copy-start
  211.8 3.2 %copy.5 = f32[2048,256]{1,0:T(8,128)} copy(f32[2048,256]{1,0:T(8,128)} %get-tuple-element.4) | data formatting | bytes 4194304
  215.0 0.0 copy-done
  215.0 1.3 copy.6
Async XLA Ops:
  211.8 3.2 %copy-start = (f32[2048,256]{1,0:T(8,128)S(1)}, f32[2048,256]{1,0:T(8,128)}, u32[]{:S(2)}) copy-start(f32[2048,256]{1,0:T(8,128)} %get-tuple-element.5) | copy-start | bytes 6291460

commit v2 on v0

v2 whole, which is shorter than its diff:
```python
import functools

import jax
import jax.numpy as jnp
from jax import lax
from jax.experimental import pallas as pl
from jax.experimental.pallas import tpu as pltpu
from jax.sharding import PartitionSpec as P

MESH = pl.DeviceIdType.MESH
F32 = jnp.float32
BF16 = jnp.bfloat16

CHUNKS = 2
W = 128
ROWS = 2048
DEPTH = 1024
SLICE = 512
SUB = 128
TILE = 512
QUARTER = 256
STEP = 256
NRECV = CHUNKS * (15 + 18 * 2)
NSEND = CHUNKS * 15
UNITS = 2
US = 512 // UNITS
UZ = 128 // UNITS


ORDER = (
    (0, "p", 0), (1, "p", 0), "split", (0, "p", 1), (0, "p", 2), (1, "p", 1), (1, "p", 2), (0, "p", 3), (0, "p", 4),
    (0, "m", 0), (1, "p", 3), (0, "u", 0, 0, 0), (0, "u", 0, 1, 0), (1, "p", 4), (0, "u", 0, 0, 1), (1, "m", 0),
    (0, "u", 0, 1, 1), (0, "u", 0, 0, 2), (1, "u", 0, 0, 0), (1, "u", 0, 1, 0), (0, "u", 0, 1, 2), (0, "u", 0, 0, 3),
    (1, "u", 0, 0, 1), (0, "u", 0, 1, 3), (1, "u", 0, 1, 1), (0, "u", 0, 0, 4), (1, "u", 0, 0, 2), (0, "u", 0, 1, 4),
    (1, "u", 0, 1, 2), (0, "u", 0, 0, 5), (1, "u", 0, 0, 3), (0, "u", 0, 1, 5), (1, "u", 0, 1, 3), (0, "s", 0, 0),
    (0, "u", 0, 0, 6), (0, "s", 1, 0), (1, "u", 0, 0, 4), (1, "u", 0, 1, 4), (0, "e", 0, 0), (0, "u", 0, 1, 6),
    (0, "s", 0, 1), (0, "e", 1, 0), (1, "u", 0, 0, 5), (0, "u", 0, 0, 7), (1, "u", 0, 1, 5), (0, "s", 1, 1),
    (0, "u", 0, 1, 7), (0, "e", 0, 1), (1, "s", 0, 0), (1, "u", 0, 0, 6), (1, "s", 1, 0), (0, "e", 1, 1), (0, "m", 1),
    (1, "e", 0, 0), (1, "u", 0, 1, 6), (1, "s", 0, 1), (1, "e", 1, 0), (1, "u", 0, 0, 7), (0, "u", 1, 0, 0),
    (0, "u", 1, 1, 0), (1, "s", 1, 1), (1, "e", 0, 1), (1, "u", 0, 1, 7), (1, "e", 1, 1), (0, "u", 1, 0, 1),
    (1, "m", 1), (0, "u", 1, 1, 1), (0, "u", 1, 0, 2), (1, "u", 1, 0, 0), (1, "u", 1, 1, 0), (0, "u", 1, 1, 2),
    (0, "u", 1, 0, 3), (1, "u", 1, 0, 1), (0, "u", 1, 1, 3), (1, "u", 1, 1, 1), (0, "u", 1, 0, 4), (1, "u", 1, 0, 2),
    (0, "u", 1, 1, 4), (1, "u", 1, 1, 2), (0, "u", 1, 0, 5), (1, "u", 1, 0, 3), (0, "u", 1, 1, 5), (1, "u", 1, 1, 3),
    (0, "u", 1, 0, 6), (1, "u", 1, 0, 4), (1, "u", 1, 1, 4), (0, "u", 1, 1, 6), (1, "u", 1, 0, 5), (0, "u", 1, 0, 7),
    (1, "u", 1, 1, 5), (0, "u", 1, 1, 7), (1, "u", 1, 0, 6), (1, "u", 1, 1, 6), (1, "u", 1, 0, 7), (1, "u", 1, 1, 7),
)


class Sems:
    def __init__(self, send, recv, anyone):
        self.send, self.recv, self.anyone, self.n_send, self.n_recv = send, recv, anyone, 0, 0

    def new_send(self):
        self.n_send += 1
        assert self.n_send <= NSEND
        return self.n_send - 1

    def new_recv(self):
        self.n_recv += 1
        assert self.n_recv <= NRECV
        return self.n_recv - 1

    def copy(self, src, dst, sent, got, device):
        return pltpu.make_async_remote_copy(
            src_ref=src,
            dst_ref=dst,
            send_sem=self.send.at[sent],
            recv_sem=self.recv.at[got],
            device_id=device,
            device_id_type=MESH,
        )

    def got(self, ref, slot):
        self.copy(ref, ref, 0, slot, self.anyone).wait_recv()

    def sent(self, ref, slot):
        self.copy(ref, ref, slot, 0, self.anyone).wait_send()


def kernel(
    x_hbm, s_hbm, n_hbm,
    xf, xs, pb, px, pr, py, pc, sc, hl, part, rx1, rx2, rz1, rz2, full,
    send_sem, recv_sem, load_sem, panel_sem, out_sem,
):
    layer = lax.axis_index("layer")
    row = lax.axis_index("row")
    col = lax.axis_index("col")
    y, q = lax.div(row, 2), lax.rem(row, 2)
    zh, x = lax.div(col, 4), lax.rem(col, 4)
    owner_core = lax.div(x, 2)
    half = lax.rem(x, 2)

    def m8(value, n):
        return pl.ds(pl.multiple_of(value, 16), n)

    def at_x(d):
        return {"col": zh * 4 + lax.rem(x + d, 4)}

    def at_z(d):
        return {"col": lax.rem(zh + d, 4) * 4 + x}

    def at_y(d):
        return {"row": lax.rem(y + d, 4) * 2 + q}

    partner = {"row": y * 2 + 1 - q}
    sems = Sems(send_sem, recv_sem, partner)
    fetches = q == owner_core
    has_panel = col == 0
    holds = jnp.logical_and(zh == 0, fetches)
    source_0 = jnp.logical_and(has_panel, q == 0)
    source_1 = jnp.logical_and(has_panel, q == 1)
    relay_1 = jnp.logical_and(jnp.logical_and(zh == 0, q == 1), x == 1)
    relay_3 = jnp.logical_and(jnp.logical_and(zh == 0, q == 1), x == 3)

    loads = [
        pltpu.make_async_copy(
            x_hbm.at[pl.ds(i * STEP, STEP), :], xf.at[pl.ds(i * STEP, STEP), :], load_sem.at[i]
        )
        for i in range(ROWS // STEP)
    ]
    panel_loads = [
        pltpu.make_async_copy(
            x_hbm.at[:, pl.ds(pl.multiple_of(layer * (CHUNKS * W) + k * W, W), W)],
            pb.at[k],
            panel_sem.at[k],
        )
        for k in range(CHUNKS)
    ]

    @pl.when(has_panel)
    def _():
        for load in panel_loads:
            load.start()

    for load in loads:
        load.start()

    barrier = pltpu.get_barrier_semaphore()
    greeted = [at_x(1), at_x(3), partner] + [at(d) for at in (at_z, at_y) for d in (1, 2, 3)]
    for device in greeted:
        pl.semaphore_signal(barrier, inc=1, device_id=device, device_id_type=MESH)
    pl.semaphore_wait(barrier, len(greeted))

    def owned(d):
        u = lax.rem(x + d - 2 * q + 4, 4)
        return (2 * lax.rem(lax.div(u + 1, 2), 2) + lax.div(u, 2)) * SLICE

    x_rows = [owned(d) for d in range(4)]

    def z_rows(d):
        return x_rows[0] + lax.rem(zh + d, 4) * SUB

    def reduce_start(buf, r1, rows, size, at, sent, got):
        h = size // 2
        sems.copy(buf.at[m8(rows[2], h)], r1.at[0], sent, got, at(1)).start()
        sems.copy(buf.at[m8(rows[2] + h, h)], r1.at[1], sent, got, at(3)).start()

    def reduce_own(buf, r2, rows, size, at, sent, got):
        h = size // 2
        sems.copy(buf.at[m8(rows[1] + h, h)], r2.at[0, pl.ds(h, h)], sent, got, at(1)).start()
        sems.copy(buf.at[m8(rows[3], h)], r2.at[1, pl.ds(0, h)], sent, got, at(3)).start()

    def reduce_middle(buf, r1, r2, rows, size, at, sent, first, got):
        h = size // 2
        sems.got(r1, first)
        buf[m8(rows[1], h)] += r1[0]
        sems.copy(buf.at[m8(rows[1], h)], r2.at[0, pl.ds(0, h)], sent, got, at(1)).start()
        buf[m8(rows[3] + h, h)] += r1[1]
        sems.copy(buf.at[m8(rows[3] + h, h)], r2.at[1, pl.ds(h, h)], sent, got, at(3)).start()

    def gather_start(buf, rows, size, at, sent, got):
        own = buf.at[m8(rows[0], size)]
        sems.copy(own, own, sent, got, at(1)).start()
        sems.copy(own, own, sent, got, at(3)).start()

    def gather_middle(buf, rows, size, at, sent, first, got):
        h = size // 2
        sems.got(buf.at[pl.ds(0, 2 * size)], first)
        left, right = buf.at[m8(rows[3], h)], buf.at[m8(rows[1] + h, h)]
        sems.copy(left, left, sent, got, at(1)).start()
        sems.copy(right, right, sent, got, at(3)).start()

    def split_rhs(src, k):
        def tile(i, carry):
            rows = pl.ds(pl.multiple_of(i * TILE, TILE), TILE)
            value = src[rows, :]
            hi = value.astype(BF16)
            hl[k, rows, pl.ds(0, W)] = hi
            hl[k, rows, pl.ds(W, W)] = (value - hi.astype(F32)).astype(BF16)
            return carry

        lax.fori_loop(0, DEPTH // TILE, tile, 0)

    def product(buf, k, first_row):
        def tile(i, carry):
            start = first_row + i * TILE
            both = jnp.dot(
                xs[pl.ds(pl.multiple_of(2 * start, 2 * TILE), 2 * TILE), :],
                hl[k],
                preferred_element_type=F32,
            )
            low = both[:TILE, W:] + (both[TILE:, :W] + both[TILE:, W:])
            buf[pl.ds(pl.multiple_of(start, TILE), TILE), :] = both[:TILE, :W] + low
            return carry

        lax.fori_loop(0, SLICE // TILE, tile, 0)

    def minus_panel(buf, k, first_row):
        @pl.when(has_panel)
        def _():
            rows = m8(first_row, SLICE)
            buf[rows, :] -= 3.0 * pb[k, rows, :]

    def split_block(first, last):
        for load in loads[first:last]:
            load.wait()

        def tile(i, carry):
            value = xf[pl.ds(pl.multiple_of(i * 64, 64), 64), :]
            hi = value.astype(BF16)
            to = lax.div(i, TILE // 64) * (2 * TILE) + lax.rem(i, TILE // 64) * 64
            xs[pl.ds(pl.multiple_of(to, 64), 64), :] = hi
            xs[pl.ds(pl.multiple_of(to + TILE, 64), 64), :] = (value - hi.astype(F32)).astype(BF16)
            return carry

        lax.fori_loop(first * STEP // 64, last * STEP // 64, tile, 0)

    def chain(k):
        steps = []
        state = {}

        along_x = [sems.new_recv() for _ in range(4)]
        to_relay = [sems.new_recv() for _ in range(2)]
        scattered = [sems.new_recv() for _ in range(4)][0]
        arrive = sems.new_recv()
        ring = [None] + [sems.new_recv() for _ in range(3)]
        share = sems.new_recv()
        source_sent, relay_sent, scatter_sent, z_sent, ring_sent, share_sent = [
            sems.new_send() for _ in range(6)
        ]

        def piece(ref, i):
            return ref.at[k, pl.ds(i * QUARTER, QUARTER)]

        def from_source(i):
            return sems.copy(piece(pb, 4 + i), piece(px, i), source_sent, along_x[i], at_x(1))

        def from_source_left(i):
            return sems.copy(piece(pb, 4 + i), piece(px, i), source_sent, along_x[i], at_x(3))

        def to_relay_copy(i):
            return sems.copy(piece(pb, i), piece(pr, i % 2), source_sent, to_relay[i % 2], at_x(1 if i < 2 else 3))

        def relay_copy(i):
            return sems.copy(piece(pr, i % 2), piece(px, i), relay_sent, along_x[i], at_x(1 if i < 2 else 3))

        def scatter_copy(i):
            return sems.copy(piece(px, i), py.at[k, y], scatter_sent, scattered + y, {"row": 2 * i + q})

        def z_copy(src, s):
            return sems.copy(src, pc.at[k, mine(0)], z_sent, arrive, {"col": s * 4 + x})

        def panel_send():
            @pl.when(has_panel)
            def _():
                panel_loads[k].wait()

            @pl.when(source_0)
            def _():
                for i in range(4):
                    from_source(i).start()
                px[k] = pb[k, pl.ds(0, DEPTH)]

            @pl.when(source_1)
            def _():
                for i in (0, 2, 1, 3):
                    to_relay_copy(i).start()
                for i in range(4):
                    from_source_left(i).start()

        def panel_scatter():
            @pl.when(relay_1)
            def _():
                for i in (0, 1):
                    to_relay_copy(i).wait_recv()
                    relay_copy(i).start()

            @pl.when(relay_3)
            def _():
                for i in (2, 3):
                    to_relay_copy(i).wait_recv()
                    relay_copy(i).start()

            @pl.when(holds)
            def _():
                for i in range(4):

                    @pl.when(x != 0)
                    def _(i=i):
                        from_source(i).wait_recv()

                    @pl.when(y != i)
                    def _(i=i):
                        scatter_copy(i).start()

                    if k == 0:
                        split_block(2 * i, 2 * i + 2)

        def panel_along_z():
            @pl.when(holds)
            def _():
                for s in (2, 1, 3, 0):

                    @pl.when(y != s)
                    def _(s=s):
                        sems.got(py.at[k, s], scattered + s)
                        if s:
                            z_copy(py.at[k, s], s).start()
                        else:
                            pc[k, mine(0)] = py[k, 0]

                    @pl.when(y == s)
                    def _(s=s):
                        if s:
                            z_copy(piece(px, s), s).start()
                        else:
                            pc[k, mine(0)] = px[k, pl.ds(0, QUARTER)]

        def mine(d):
            return m8(lax.rem(y + 4 - d, 4) * QUARTER, QUARTER)

        def ring_copy(d):
            return sems.copy(pc.at[k, mine(0)], pc.at[k, mine(0)], ring_sent, ring[d], at_y(d))

        def share_copy(d):
            return sems.copy(pc.at[k, mine(d)], pc.at[k, mine(d)], share_sent, share, partner)

        def panel_ring():
            @pl.when(fetches)
            def _():
                @pl.when(zh != 0)
                def _():
                    sems.got(pc.at[k, mine(0)], arrive)

                for d in (1, 3, 2):
                    ring_copy(d).start()
                share_copy(0).start()

        def panel_share():
            @pl.when(fetches)
            def _():
                for d in (1, 3, 2):
                    ring_copy(d).wait_recv()
                    share_copy(d).start()

            @pl.when(jnp.logical_not(fetches))
            def _():
                sems.got(pc.at[k], share)

        def panel_drain():
            @pl.when(source_0)
            def _():
                sems.sent(px.at[k], source_sent)

            @pl.when(source_1)
            def _():
                sems.sent(pb.at[k], source_sent)

            @pl.when(jnp.logical_or(relay_1, relay_3))
            def _():
                sems.sent(pr.at[k], relay_sent)

            @pl.when(holds)
            def _():
                sems.sent(px.at[k, pl.ds(0, 3 * QUARTER)], scatter_sent)
                sems.sent(px.at[k, pl.ds(0, 3 * QUARTER)], z_sent)

            @pl.when(fetches)
            def _():
                sems.sent(pc.at[k, pl.ds(0, 3 * QUARTER)], ring_sent)
                sems.sent(pc.at[k], share_sent)

        def ring_drain(phase):
            x_rows_sent = part.at[phase, k, pl.ds(0, 3 * SLICE)]
            sems.sent(x_rows_sent, x_sent[phase])
            sems.sent(x_rows_sent, gx_sent[phase])
            sems.sent(part.at[phase, k, pl.ds(0, 6 * SUB)], z_ring_sent[phase])

        x_sent = [sems.new_send() for _ in range(2)]
        gx_sent = [sems.new_send() for _ in range(2)]
        z_ring_sent = [sems.new_send() for _ in range(2)]
        slots = {
            (phase, u, name): sems.new_recv()
            for phase in range(2)
            for u in range(UNITS)
            for name in ("x1", "x2", "z1", "z2", "g1", "g2", "g3", "g4")
        }

        def multiply(phase):
            buf = part.at[phase, k]

            def run(first_row):
                product(buf, k, first_row)
                if phase == 1:
                    minus_panel(buf, k, first_row)

            def step():
                split_rhs((pc if phase == 0 else sc).at[k], k)
                run(x_rows[2])
                for u in range(UNITS):
                    reduce_start(
                        buf, rx1.at[phase, k, u], unit_x[u], US, at_x, x_sent[phase], slots[phase, u, "x1"]
                    )
                run(x_rows[1])
                run(x_rows[3])
                for u in range(UNITS):
                    reduce_own(
                        buf, rx2.at[phase, k, u], unit_x[u], US, at_x, x_sent[phase], slots[phase, u, "x2"]
                    )
                run(x_rows[0])

            return step

        unit_x = [[r + u * US for r in x_rows] for u in range(UNITS)]
        unit_z = [
            [unit_x[u][0] + lax.rem(zh + d, 4) * UZ for d in range(4)] for u in range(UNITS)
        ]

        def unit_steps(phase, u):
            buf = part.at[phase, k]
            out = full.at[phase, k]
            xr, zr = unit_x[u], unit_z[u]
            xs_, zs_, gs_ = x_sent[phase], z_ring_sent[phase], gx_sent[phase]
            slot = {name: slots[phase, u, name] for name in ("x1", "x2", "z1", "z2", "g1", "g2", "g3", "g4")}

            def x_middle():
                reduce_middle(
                    buf, rx1.at[phase, k, u], rx2.at[phase, k, u], xr, US, at_x, xs_, slot["x1"], slot["x2"]
                )

            def x_end():
                sems.got(rx2.at[phase, k, u], slot["x2"])
                rows = m8(xr[0], US)
                buf[rows] += rx2[phase, k, u, 0] + rx2[phase, k, u, 1]
                reduce_start(buf, rz1.at[phase, k, u], zr, UZ, at_z, zs_, slot["z1"])
                reduce_own(buf, rz2.at[phase, k, u], zr, UZ, at_z, zs_, slot["z2"])

            def z_middle():
                reduce_middle(
                    buf, rz1.at[phase, k, u], rz2.at[phase, k, u], zr, UZ, at_z, zs_, slot["z1"], slot["z2"]
                )

            def z_end():
                sems.got(rz2.at[phase, k, u], slot["z2"])
                rows = m8(zr[0], UZ)
                total = buf[rows] + (rz2[phase, k, u, 0] + rz2[phase, k, u, 1])
                out[rows] = total if phase == 0 else total * -0.5
                gather_start(out, zr, UZ, at_z, zs_, slot["g1"])

            def gz_middle():
                gather_middle(out, zr, UZ, at_z, zs_, slot["g1"], slot["g2"])

            def gx_start():
                sems.got(out.at[pl.ds(0, UZ)], slot["g2"])
                gather_start(out, xr, US, at_x, gs_, slot["g3"])
                if phase == 0:
                    send_slab(u, 0)

            def gx_middle():
                gather_middle(out, xr, US, at_x, gs_, slot["g3"], slot["g4"])
                if phase == 0:
                    send_slab(u, 1)

            def gx_end():
                sems.got(out.at[pl.ds(0, US)], slot["g4"])
                if u == UNITS - 1:
                    store = pltpu.make_async_copy(
                        out,
                        (s_hbm if phase == 0 else n_hbm).at[:, pl.ds(k * W, W)],
                        out_sem.at[phase, k],
                    )
                    store.start()
                    state[phase, "store"] = store

            return [x_middle, x_end, z_middle, z_end, gz_middle, gx_start, gx_middle, gx_end]

        turn = lax.rem(y - zh + 4, 4)
        root = jnp.logical_and(fetches, turn == 0)
        y1 = jnp.logical_and(fetches, turn == 1)
        y2 = jnp.logical_and(fetches, turn == 2)
        y3 = jnp.logical_and(fetches, turn == 3)
        fwd = {(i, u): sems.new_recv() for i in range(2) for u in range(UNITS)}
        root_sent, onward_sent, across_sent = [sems.new_send() for _ in range(3)]

        def held(i, u):
            return full.at[0, k, m8(half * DEPTH + i * SLICE + u * US, US)]

        def block(i, u):
            return sc.at[k, pl.ds(i * SLICE + u * US, US)]

        def from_root(i, u, d):
            return sems.copy(held(i, u), block(i, u), root_sent, fwd[i, u], at_y(d))

        def onward(i, u):
            return sems.copy(block(i, u), block(i, u), onward_sent, fwd[i, u], at_y(1 + 2 * i))

        def across(i, u):
            return sems.copy(block(i, u), block(i, u), across_sent, fwd[i, u], partner)

        def send_slab(u, i):
            @pl.when(root)
            def _():
                from_root(i, u, 1).start()
                from_root(i, u, 3).start()
                block(i, u)[...] = held(i, u)[...]
                across(i, u).start()

        def pass_slab(u, i):
            def step():
                for d, here in ((1, y1), (3, y3)):

                    @pl.when(here)
                    def _(d=d):
                        from_root(i, u, d).wait_recv()
                        if d == 1 + 2 * i:
                            onward(i, u).start()
                        across(i, u).start()

            return step

        def end_slab(u, i):
            def step():
                @pl.when(y2)
                def _():
                    onward(i, u).wait_recv()
                    across(i, u).start()

                @pl.when(jnp.logical_not(fetches))
                def _():
                    across(i, u).wait_recv()

            return step

        pieces = [(u, i) for u in range(UNITS) for i in range(2)]

        def slab_drain():
            @pl.when(root)
            def _():
                sems.sent(full.at[0, k], root_sent)

            @pl.when(jnp.logical_or(y1, y3))
            def _():
                sems.sent(sc.at[k, pl.ds(0, SLICE)], onward_sent)

            @pl.when(fetches)
            def _():
                sems.sent(sc.at[k], across_sent)

            ring_drain(0)
            ring_drain(1)

        panel = [panel_send, panel_scatter, panel_along_z, panel_ring, panel_share]
        named = {("p", i): f for i, f in enumerate(panel)}
        named["m", 0], named["m", 1] = multiply(0), multiply(1)
        for phase in range(2):
            for u in range(UNITS):
                for i, f in enumerate(unit_steps(phase, u)):
                    named["u", phase, u, i] = f
        for u, i in pieces:
            named["s", u, i] = pass_slab(u, i)
            named["e", u, i] = end_slab(u, i)
        return named, [panel_drain, slab_drain], state

    chains = [chain(k) for k in range(CHUNKS)]
    for step in ORDER:
        if step == "split":

            @pl.when(jnp.logical_not(holds))
            def _():
                split_block(0, ROWS // STEP)
        else:
            chains[step[0]][0][step[1:]]()
    for _, ends, state in chains:
        for end in ends:
            end()
        for phase in range(2):
            state[phase, "store"].wait()


def solution(mesh):
    def body(matrix):
        return pl.pallas_call(
            kernel,
            out_shape=(
                jax.ShapeDtypeStruct((ROWS, CHUNKS * W), F32),
                jax.ShapeDtypeStruct((ROWS, CHUNKS * W), F32),
            ),
            in_specs=[pl.BlockSpec(memory_space=pl.ANY)],
            out_specs=(pl.BlockSpec(memory_space=pl.ANY), pl.BlockSpec(memory_space=pl.ANY)),
            scratch_shapes=[
                pltpu.VMEM((ROWS, DEPTH), F32),
                pltpu.VMEM((2 * ROWS, DEPTH), BF16),
                pltpu.VMEM((CHUNKS, ROWS, W), F32),
                pltpu.VMEM((CHUNKS, DEPTH, W), F32),
                pltpu.VMEM((CHUNKS, 2 * QUARTER, W), F32),
                pltpu.VMEM((CHUNKS, 4, QUARTER, W), F32),
                pltpu.VMEM((CHUNKS, DEPTH, W), F32),
                pltpu.VMEM((CHUNKS, DEPTH, W), F32),
                pltpu.VMEM((CHUNKS, DEPTH, 2 * W), BF16),
                pltpu.VMEM((2, CHUNKS, ROWS, W), F32),
                pltpu.VMEM((2, CHUNKS, UNITS, 2, US // 2, W), F32),
                pltpu.VMEM((2, CHUNKS, UNITS, 2, US, W), F32),
                pltpu.VMEM((2, CHUNKS, UNITS, 2, UZ // 2, W), F32),
                pltpu.VMEM((2, CHUNKS, UNITS, 2, UZ, W), F32),
                pltpu.VMEM((2, CHUNKS, ROWS, W), F32),
                pltpu.SemaphoreType.DMA((NSEND,)),
                pltpu.SemaphoreType.DMA((NRECV,)),
                pltpu.SemaphoreType.DMA((ROWS // STEP,)),
                pltpu.SemaphoreType.DMA((CHUNKS,)),
                pltpu.SemaphoreType.DMA((2, CHUNKS)),
            ],
            compiler_params=pltpu.CompilerParams(
                collective_id=0, has_side_effects=True, vmem_limit_bytes=60 * 1024 * 1024
            ),
        )(matrix)

    return jax.shard_map(
        body,
        mesh=mesh,
        in_specs=(P("row", "col"),),
        out_specs=(P("row", "layer"), P("row", "layer")),
        check_vma=False,
    )
```

time: 810 us -> 148 us (0.18)
  waiting for transfers between devices: 759 us -> 0 us
  Pallas kernels: 0 us -> 141 us
  matrix products: 20.1 us -> 0 us
  between operations: 14.2 us -> 0.65 us
  other arithmetic: 13 us -> 0 us
    psum x5 -> x0, waiting for transfers between devices: 696 us -> none  [the longest x3 348 us: from_root(): return lax.psum(jnp.where(mine, shard, jnp.zeros_like(shard)), axis)]
    pallas_call x0 -> x1, Pallas kernels: none -> 141 us  [body(): pl.pallas_call(kernel, out_shape=(jax.ShapeDtypeStruct((ROWS, CHUNKS * W)...]
    reduce_scatter x1 -> x0, waiting for transfers between devices: 62.9 us -> none  [body(): lax.psum_scatter(matmul_high(local_cols, square_slab), 'layer', scatter_d...]
    dot_general x2 -> x0, matrix products: 20.1 us -> none  [matmul_high(): jnp.dot(left_side, right_side, precision=lax.Precision.HIGHEST, preferred...]
    select_n x3 -> x0, other arithmetic: 9.22 us -> none  [from_root(): return lax.psum(jnp.where(mine, shard, jnp.zeros_like(shard)), axis)]
  transfers between devices with their start and end apart: 6 -> 0, of which waited for: 6 -> 0; matrix products, arithmetic and copies ran while one was open for 0% -> 0% of each run, Pallas kernels for 0% -> 0%
where the time goes in v2:
time: 148 us; the launch traced here: 147 us
  Pallas kernels  141 us (95%)
  local copies, waits for them, and re-layouts  4.52 us (3%)
    pallas_call x1, Pallas kernels, body(): pl.pallas_call(kernel, out_shape=(jax.ShapeDtypeStruct((ROWS, CHUNKS * W)...  141 us
    unnamed x4, local copies, waits for them, and re-layouts  4.52 us

profile of v2, /device:TPU:16, one launch (start us, length us, event | category | flops | bytes accessed | tf_op | source)
XLA Modules:
  0.0 146.7 jit_solution(4922057258912578677)
XLA Ops:
  0.6 141.5 %shard_map.30 = (f32[2048,256]{1,0:T(8,128)}, f32[2048,256]{1,0:T(8,128)}) custom-call(f32[2048,1024]{1,0:T(8,128)} %x_hbm.1), custom_call_target="tpu_custom_call" | custom-call | tf_op jit(solution)/shard_map/pallas_call | solution.py:592
  142.1 0.0 copy-start
  142.1 3.2 %copy.5 = f32[2048,256]{1,0:T(8,128)} copy(f32[2048,256]{1,0:T(8,128)} %get-tuple-element.4) | data formatting | bytes 4194304
  145.3 0.0 copy-done
  145.3 1.3 copy.6
Async XLA Ops:
  142.1 3.2 %copy-start = (f32[2048,256]{1,0:T(8,128)S(1)}, f32[2048,256]{1,0:T(8,128)}, u32[]{:S(2)}) copy-start(f32[2048,256]{1,0:T(8,128)} %get-tuple-element.5) | copy-start | bytes 6291460

commit v3 on v2

--- a/solution.py
+++ b/solution.py
@@ -20,29 +20,43 @@
 TILE = 512
 QUARTER = 256
 STEP = 256
-NRECV = CHUNKS * (15 + 18 * 2)
+NRECV = CHUNKS * (15 + 18 * 4)
 NSEND = CHUNKS * 15
-UNITS = 2
+UNITS = 4
 US = 512 // UNITS
 UZ = 128 // UNITS
 
 
 ORDER = (
     (0, "p", 0), (1, "p", 0), "split", (0, "p", 1), (0, "p", 2), (1, "p", 1), (1, "p", 2), (0, "p", 3), (0, "p", 4),
-    (0, "m", 0), (1, "p", 3), (0, "u", 0, 0, 0), (0, "u", 0, 1, 0), (1, "p", 4), (0, "u", 0, 0, 1), (1, "m", 0),
-    (0, "u", 0, 1, 1), (0, "u", 0, 0, 2), (1, "u", 0, 0, 0), (1, "u", 0, 1, 0), (0, "u", 0, 1, 2), (0, "u", 0, 0, 3),
-    (1, "u", 0, 0, 1), (0, "u", 0, 1, 3), (1, "u", 0, 1, 1), (0, "u", 0, 0, 4), (1, "u", 0, 0, 2), (0, "u", 0, 1, 4),
-    (1, "u", 0, 1, 2), (0, "u", 0, 0, 5), (1, "u", 0, 0, 3), (0, "u", 0, 1, 5), (1, "u", 0, 1, 3), (0, "s", 0, 0),
-    (0, "u", 0, 0, 6), (0, "s", 1, 0), (1, "u", 0, 0, 4), (1, "u", 0, 1, 4), (0, "e", 0, 0), (0, "u", 0, 1, 6),
-    (0, "s", 0, 1), (0, "e", 1, 0), (1, "u", 0, 0, 5), (0, "u", 0, 0, 7), (1, "u", 0, 1, 5), (0, "s", 1, 1),
-    (0, "u", 0, 1, 7), (0, "e", 0, 1), (1, "s", 0, 0), (1, "u", 0, 0, 6), (1, "s", 1, 0), (0, "e", 1, 1), (0, "m", 1),
-    (1, "e", 0, 0), (1, "u", 0, 1, 6), (1, "s", 0, 1), (1, "e", 1, 0), (1, "u", 0, 0, 7), (0, "u", 1, 0, 0),
-    (0, "u", 1, 1, 0), (1, "s", 1, 1), (1, "e", 0, 1), (1, "u", 0, 1, 7), (1, "e", 1, 1), (0, "u", 1, 0, 1),
-    (1, "m", 1), (0, "u", 1, 1, 1), (0, "u", 1, 0, 2), (1, "u", 1, 0, 0), (1, "u", 1, 1, 0), (0, "u", 1, 1, 2),
-    (0, "u", 1, 0, 3), (1, "u", 1, 0, 1), (0, "u", 1, 1, 3), (1, "u", 1, 1, 1), (0, "u", 1, 0, 4), (1, "u", 1, 0, 2),
-    (0, "u", 1, 1, 4), (1, "u", 1, 1, 2), (0, "u", 1, 0, 5), (1, "u", 1, 0, 3), (0, "u", 1, 1, 5), (1, "u", 1, 1, 3),
-    (0, "u", 1, 0, 6), (1, "u", 1, 0, 4), (1, "u", 1, 1, 4), (0, "u", 1, 1, 6), (1, "u", 1, 0, 5), (0, "u", 1, 0, 7),
-    (1, "u", 1, 1, 5), (0, "u", 1, 1, 7), (1, "u", 1, 0, 6), (1, "u", 1, 1, 6), (1, "u", 1, 0, 7), (1, "u", 1, 1, 7),
+    (0, "m", 0), (1, "p", 3), (0, "u", 0, 0, 0), (0, "u", 0, 1, 0), (0, "u", 0, 2, 0), (0, "u", 0, 3, 0), (1, "p", 4),
+    (0, "u", 0, 0, 1), (0, "u", 0, 1, 1), (1, "m", 0), (0, "u", 0, 2, 1), (0, "u", 0, 3, 1), (0, "u", 0, 0, 2),
+    (0, "u", 0, 1, 2), (1, "u", 0, 0, 0), (1, "u", 0, 1, 0), (1, "u", 0, 2, 0), (1, "u", 0, 3, 0), (0, "u", 0, 2, 2),
+    (0, "u", 0, 3, 2), (0, "u", 0, 0, 3), (0, "u", 0, 1, 3), (1, "u", 0, 0, 1), (1, "u", 0, 1, 1), (1, "u", 0, 2, 1),
+    (0, "u", 0, 2, 3), (1, "u", 0, 3, 1), (0, "u", 0, 3, 3), (0, "u", 0, 0, 4), (0, "u", 0, 1, 4), (1, "u", 0, 0, 2),
+    (1, "u", 0, 1, 2), (1, "u", 0, 2, 2), (0, "u", 0, 2, 4), (1, "u", 0, 3, 2), (0, "u", 0, 3, 4), (0, "u", 0, 0, 5),
+    (0, "u", 0, 1, 5), (1, "u", 0, 0, 3), (1, "u", 0, 1, 3), (1, "u", 0, 2, 3), (0, "u", 0, 2, 5), (1, "u", 0, 3, 3),
+    (0, "s", 0, 0), (0, "u", 0, 3, 5), (0, "s", 1, 0), (0, "u", 0, 0, 6), (0, "s", 2, 0), (1, "u", 0, 0, 4),
+    (0, "u", 0, 1, 6), (0, "e", 0, 0), (1, "u", 0, 1, 4), (0, "s", 3, 0), (0, "e", 1, 0), (1, "u", 0, 2, 4),
+    (0, "s", 0, 1), (0, "u", 0, 2, 6), (1, "u", 0, 3, 4), (0, "e", 2, 0), (0, "s", 1, 1), (0, "u", 0, 3, 6),
+    (1, "u", 0, 0, 5), (0, "e", 3, 0), (0, "u", 0, 0, 7), (1, "u", 0, 1, 5), (0, "e", 0, 1), (0, "s", 2, 1),
+    (0, "u", 0, 1, 7), (1, "u", 0, 2, 5), (0, "u", 0, 2, 7), (1, "u", 0, 3, 5), (0, "e", 1, 1), (0, "s", 3, 1),
+    (0, "u", 0, 3, 7), (1, "s", 0, 0), (0, "e", 2, 1), (1, "s", 1, 0), (1, "u", 0, 0, 6), (1, "s", 2, 0),
+    (0, "e", 3, 1), (1, "s", 3, 0), (1, "u", 0, 1, 6), (1, "e", 0, 0), (0, "m", 1), (1, "e", 1, 0), (1, "s", 0, 1),
+    (1, "u", 0, 2, 6), (1, "e", 2, 0), (1, "e", 3, 0), (1, "s", 1, 1), (1, "u", 0, 3, 6), (1, "u", 0, 0, 7),
+    (1, "u", 0, 1, 7), (0, "u", 1, 0, 0), (0, "u", 1, 1, 0), (0, "u", 1, 2, 0), (0, "u", 1, 3, 0), (1, "e", 0, 1),
+    (1, "s", 2, 1), (1, "e", 1, 1), (1, "s", 3, 1), (1, "e", 2, 1), (1, "u", 0, 2, 7), (1, "e", 3, 1),
+    (1, "u", 0, 3, 7), (0, "u", 1, 0, 1), (1, "m", 1), (0, "u", 1, 1, 1), (0, "u", 1, 2, 1), (0, "u", 1, 3, 1),
+    (0, "u", 1, 0, 2), (1, "u", 1, 0, 0), (1, "u", 1, 1, 0), (1, "u", 1, 2, 0), (1, "u", 1, 3, 0), (0, "u", 1, 1, 2),
+    (0, "u", 1, 2, 2), (0, "u", 1, 3, 2), (1, "u", 1, 0, 1), (0, "u", 1, 0, 3), (1, "u", 1, 1, 1), (1, "u", 1, 2, 1),
+    (0, "u", 1, 1, 3), (1, "u", 1, 3, 1), (0, "u", 1, 2, 3), (0, "u", 1, 3, 3), (1, "u", 1, 0, 2), (0, "u", 1, 0, 4),
+    (1, "u", 1, 1, 2), (1, "u", 1, 2, 2), (0, "u", 1, 1, 4), (1, "u", 1, 3, 2), (0, "u", 1, 2, 4), (0, "u", 1, 3, 4),
+    (1, "u", 1, 0, 3), (0, "u", 1, 0, 5), (1, "u", 1, 1, 3), (1, "u", 1, 2, 3), (0, "u", 1, 1, 5), (1, "u", 1, 3, 3),
+    (0, "u", 1, 2, 5), (0, "u", 1, 3, 5), (1, "u", 1, 0, 4), (0, "u", 1, 0, 6), (1, "u", 1, 1, 4), (1, "u", 1, 2, 4),
+    (0, "u", 1, 1, 6), (1, "u", 1, 3, 4), (0, "u", 1, 2, 6), (1, "u", 1, 0, 5), (1, "u", 1, 1, 5), (0, "u", 1, 3, 6),
+    (1, "u", 1, 2, 5), (0, "u", 1, 0, 7), (1, "u", 1, 3, 5), (0, "u", 1, 1, 7), (0, "u", 1, 2, 7), (1, "u", 1, 0, 6),
+    (1, "u", 1, 1, 6), (0, "u", 1, 3, 7), (1, "u", 1, 2, 6), (1, "u", 1, 3, 6), (1, "u", 1, 0, 7), (1, "u", 1, 1, 7),
+    (1, "u", 1, 2, 7), (1, "u", 1, 3, 7),
 )
 
 
@@ -78,10 +92,11 @@
 
 
 def kernel(
-    x_hbm, s_hbm, n_hbm,
-    xf, xs, pb, px, pr, py, pc, sc, hl, part, rx1, rx2, rz1, rz2, full,
-    send_sem, recv_sem, load_sem, panel_sem, out_sem,
+    x_hbm, s_out, n_out,
+    xf, xs, pb, px, pr, py, pc, sc, hl, part, rx1, rx2, rz1, rz2,
+    send_sem, recv_sem, load_sem, panel_sem,
 ):
+    outs = (s_out, n_out)
     layer = lax.axis_index("layer")
     row = lax.axis_index("row")
     col = lax.axis_index("col")
@@ -342,7 +357,7 @@
                 def _():
                     sems.got(pc.at[k, mine(0)], arrive)
 
-                for d in (1, 3, 2):
+                for d in (2, 1, 3):
                     ring_copy(d).start()
                 share_copy(0).start()
 
@@ -428,7 +443,7 @@
 
         def unit_steps(phase, u):
             buf = part.at[phase, k]
-            out = full.at[phase, k]
+            out = outs[phase].at[k]
             xr, zr = unit_x[u], unit_z[u]
             xs_, zs_, gs_ = x_sent[phase], z_ring_sent[phase], gx_sent[phase]
             slot = {name: slots[phase, u, name] for name in ("x1", "x2", "z1", "z2", "g1", "g2", "g3", "g4")}
@@ -473,14 +488,6 @@
 
             def gx_end():
                 sems.got(out.at[pl.ds(0, US)], slot["g4"])
-                if u == UNITS - 1:
-                    store = pltpu.make_async_copy(
-                        out,
-                        (s_hbm if phase == 0 else n_hbm).at[:, pl.ds(k * W, W)],
-                        out_sem.at[phase, k],
-                    )
-                    store.start()
-                    state[phase, "store"] = store
 
             return [x_middle, x_end, z_middle, z_end, gz_middle, gx_start, gx_middle, gx_end]
 
@@ -493,7 +500,7 @@
         root_sent, onward_sent, across_sent = [sems.new_send() for _ in range(3)]
 
         def held(i, u):
-            return full.at[0, k, m8(half * DEPTH + i * SLICE + u * US, US)]
+            return outs[0].at[k, m8(half * DEPTH + i * SLICE + u * US, US)]
 
         def block(i, u):
             return sc.at[k, pl.ds(i * SLICE + u * US, US)]
@@ -546,7 +553,7 @@
         def slab_drain():
             @pl.when(root)
             def _():
-                sems.sent(full.at[0, k], root_sent)
+                sems.sent(outs[0].at[k], root_sent)
 
             @pl.when(jnp.logical_or(y1, y3))
             def _():
@@ -583,20 +590,30 @@
     for _, ends, state in chains:
         for end in ends:
             end()
-        for phase in range(2):
-            state[phase, "store"].wait()
+
+
+def lay_out(square, new, square_out, new_out, sem):
+    copies = [
+        pltpu.make_async_copy(src.at[k], dst.at[:, pl.ds(k * W, W)], sem.at[i, k])
+        for i, (src, dst) in enumerate(((square, square_out), (new, new_out)))
+        for k in range(CHUNKS)
+    ]
+    for copy in copies:
+        copy.start()
+    for copy in copies:
+        copy.wait()
 
 
 def solution(mesh):
     def body(matrix):
-        return pl.pallas_call(
+        square, new = pl.pallas_call(
             kernel,
             out_shape=(
-                jax.ShapeDtypeStruct((ROWS, CHUNKS * W), F32),
-                jax.ShapeDtypeStruct((ROWS, CHUNKS * W), F32),
+                pltpu.VMEM((CHUNKS, ROWS, W), F32),
+                pltpu.VMEM((CHUNKS, ROWS, W), F32),
             ),
             in_specs=[pl.BlockSpec(memory_space=pl.ANY)],
-            out_specs=(pl.BlockSpec(memory_space=pl.ANY), pl.BlockSpec(memory_space=pl.ANY)),
+            out_specs=(pl.BlockSpec(memory_space=pltpu.VMEM), pl.BlockSpec(memory_space=pltpu.VMEM)),
             scratch_shapes=[
                 pltpu.VMEM((ROWS, DEPTH), F32),
                 pltpu.VMEM((2 * ROWS, DEPTH), BF16),
@@ -612,17 +629,25 @@
                 pltpu.VMEM((2, CHUNKS, UNITS, 2, US, W), F32),
                 pltpu.VMEM((2, CHUNKS, UNITS, 2, UZ // 2, W), F32),
                 pltpu.VMEM((2, CHUNKS, UNITS, 2, UZ, W), F32),
-                pltpu.VMEM((2, CHUNKS, ROWS, W), F32),
                 pltpu.SemaphoreType.DMA((NSEND,)),
                 pltpu.SemaphoreType.DMA((NRECV,)),
                 pltpu.SemaphoreType.DMA((ROWS // STEP,)),
                 pltpu.SemaphoreType.DMA((CHUNKS,)),
-                pltpu.SemaphoreType.DMA((2, CHUNKS)),
             ],
             compiler_params=pltpu.CompilerParams(
-                collective_id=0, has_side_effects=True, vmem_limit_bytes=60 * 1024 * 1024
+                collective_id=0, has_side_effects=True, vmem_limit_bytes=52 * 1024 * 1024
             ),
         )(matrix)
+        whole = jax.ShapeDtypeStruct((ROWS, CHUNKS * W), F32)
+        anywhere = pl.BlockSpec(memory_space=pl.ANY)
+        return pl.pallas_call(
+            lay_out,
+            out_shape=(whole, whole),
+            in_specs=[anywhere, anywhere],
+            out_specs=(anywhere, anywhere),
+            scratch_shapes=[pltpu.SemaphoreType.DMA((2, CHUNKS))],
+            compiler_params=pltpu.CompilerParams(vmem_limit_bytes=1024 * 1024),
+        )(square, new)
 
     return jax.shard_map(
         body,

time: 148 us -> 140 us (0.946)
  local copies, waits for them, and re-layouts: 4.52 us -> 0 us
  Pallas kernels: 141 us -> 139 us
    unnamed x4 -> x0, local copies, waits for them, and re-layouts: 4.52 us -> none
    pallas_call x1 -> x2, Pallas kernels: 141 us -> 139 us  [the longest x1 137 us: body(): pl.pallas_call(kernel, out_shape=(pltpu.VMEM((CHUNKS, ROWS, W), F32), plt...]
where the time goes in v3:
time: 140 us
  Pallas kernels  139 us (99%)
    pallas_call x1, Pallas kernels, body(): pl.pallas_call(kernel, out_shape=(pltpu.VMEM((CHUNKS, ROWS, W), F32), plt...  137 us

profile of v3, /device:TPU:16, one launch (start us, length us, event | category | flops | bytes accessed | tf_op | source)
XLA Modules:
  0.0 139.7 jit_solution(4763339981501337499)
XLA Ops:
  0.6 137.0 %shard_map.30 = (f32[2,2048,128]{2,1,0:T(8,128)S(1)}, f32[2,2048,128]{2,1,0:T(8,128)S(1)}) custom-call(f32[2048,1024]{1,0:T(8,128)} %x_hbm.1), custom_call_target="tpu_custom_call" | custom-call | tf_op jit(solution)/shard_map/pallas_call | solution.py:609
  137.6 2.0 %shard_map.31 = (f32[2048,256]{1,0:T(8,128)}, f32[2048,256]{1,0:T(8,128)}) custom-call(f32[2,2048,128]{2,1,0:T(8,128)S(1)} %get-tuple-element.4.square, f32[2,2048,128]{2,1,0:T(8,128)S(1)} %get-tuple-element.5.new), custom_call_target="tpu_custom_call" | custom-call | tf_op jit(solution)/shard_map/pallas_call | solution.py:643

commit v4 on v3

--- a/solution.py
+++ b/solution.py
@@ -39,24 +39,25 @@
     (0, "s", 0, 0), (0, "u", 0, 3, 5), (0, "s", 1, 0), (0, "u", 0, 0, 6), (0, "s", 2, 0), (1, "u", 0, 0, 4),
     (0, "u", 0, 1, 6), (0, "e", 0, 0), (1, "u", 0, 1, 4), (0, "s", 3, 0), (0, "e", 1, 0), (1, "u", 0, 2, 4),
     (0, "s", 0, 1), (0, "u", 0, 2, 6), (1, "u", 0, 3, 4), (0, "e", 2, 0), (0, "s", 1, 1), (0, "u", 0, 3, 6),
-    (1, "u", 0, 0, 5), (0, "e", 3, 0), (0, "u", 0, 0, 7), (1, "u", 0, 1, 5), (0, "e", 0, 1), (0, "s", 2, 1),
-    (0, "u", 0, 1, 7), (1, "u", 0, 2, 5), (0, "u", 0, 2, 7), (1, "u", 0, 3, 5), (0, "e", 1, 1), (0, "s", 3, 1),
-    (0, "u", 0, 3, 7), (1, "s", 0, 0), (0, "e", 2, 1), (1, "s", 1, 0), (1, "u", 0, 0, 6), (1, "s", 2, 0),
-    (0, "e", 3, 1), (1, "s", 3, 0), (1, "u", 0, 1, 6), (1, "e", 0, 0), (0, "m", 1), (1, "e", 1, 0), (1, "s", 0, 1),
-    (1, "u", 0, 2, 6), (1, "e", 2, 0), (1, "e", 3, 0), (1, "s", 1, 1), (1, "u", 0, 3, 6), (1, "u", 0, 0, 7),
-    (1, "u", 0, 1, 7), (0, "u", 1, 0, 0), (0, "u", 1, 1, 0), (0, "u", 1, 2, 0), (0, "u", 1, 3, 0), (1, "e", 0, 1),
-    (1, "s", 2, 1), (1, "e", 1, 1), (1, "s", 3, 1), (1, "e", 2, 1), (1, "u", 0, 2, 7), (1, "e", 3, 1),
-    (1, "u", 0, 3, 7), (0, "u", 1, 0, 1), (1, "m", 1), (0, "u", 1, 1, 1), (0, "u", 1, 2, 1), (0, "u", 1, 3, 1),
-    (0, "u", 1, 0, 2), (1, "u", 1, 0, 0), (1, "u", 1, 1, 0), (1, "u", 1, 2, 0), (1, "u", 1, 3, 0), (0, "u", 1, 1, 2),
-    (0, "u", 1, 2, 2), (0, "u", 1, 3, 2), (1, "u", 1, 0, 1), (0, "u", 1, 0, 3), (1, "u", 1, 1, 1), (1, "u", 1, 2, 1),
-    (0, "u", 1, 1, 3), (1, "u", 1, 3, 1), (0, "u", 1, 2, 3), (0, "u", 1, 3, 3), (1, "u", 1, 0, 2), (0, "u", 1, 0, 4),
-    (1, "u", 1, 1, 2), (1, "u", 1, 2, 2), (0, "u", 1, 1, 4), (1, "u", 1, 3, 2), (0, "u", 1, 2, 4), (0, "u", 1, 3, 4),
-    (1, "u", 1, 0, 3), (0, "u", 1, 0, 5), (1, "u", 1, 1, 3), (1, "u", 1, 2, 3), (0, "u", 1, 1, 5), (1, "u", 1, 3, 3),
-    (0, "u", 1, 2, 5), (0, "u", 1, 3, 5), (1, "u", 1, 0, 4), (0, "u", 1, 0, 6), (1, "u", 1, 1, 4), (1, "u", 1, 2, 4),
-    (0, "u", 1, 1, 6), (1, "u", 1, 3, 4), (0, "u", 1, 2, 6), (1, "u", 1, 0, 5), (1, "u", 1, 1, 5), (0, "u", 1, 3, 6),
-    (1, "u", 1, 2, 5), (0, "u", 1, 0, 7), (1, "u", 1, 3, 5), (0, "u", 1, 1, 7), (0, "u", 1, 2, 7), (1, "u", 1, 0, 6),
-    (1, "u", 1, 1, 6), (0, "u", 1, 3, 7), (1, "u", 1, 2, 6), (1, "u", 1, 3, 6), (1, "u", 1, 0, 7), (1, "u", 1, 1, 7),
-    (1, "u", 1, 2, 7), (1, "u", 1, 3, 7),
+    (1, "u", 0, 0, 5), (0, "e", 3, 0), (1, "u", 0, 1, 5), (0, "e", 0, 1), (0, "s", 2, 1), (1, "u", 0, 2, 5),
+    (1, "u", 0, 3, 5), (0, "e", 1, 1), (0, "s", 3, 1), (1, "s", 0, 0), (0, "e", 2, 1), (1, "s", 1, 0),
+    (1, "u", 0, 0, 6), (1, "s", 2, 0), (0, "e", 3, 1), (1, "s", 3, 0), (1, "u", 0, 1, 6), (1, "e", 0, 0), (0, "m", 1),
+    (1, "e", 1, 0), (1, "s", 0, 1), (1, "u", 0, 2, 6), (1, "e", 2, 0), (1, "e", 3, 0), (1, "s", 1, 1),
+    (1, "u", 0, 3, 6), (0, "u", 1, 0, 0), (0, "u", 1, 1, 0), (0, "u", 1, 2, 0), (0, "u", 1, 3, 0), (1, "e", 0, 1),
+    (1, "s", 2, 1), (1, "e", 1, 1), (1, "s", 3, 1), (1, "e", 2, 1), (1, "e", 3, 1), (0, "u", 1, 0, 1), (1, "m", 1),
+    (0, "u", 1, 1, 1), (0, "u", 1, 2, 1), (0, "u", 1, 3, 1), (0, "u", 0, 0, 8), (0, "u", 0, 1, 8), (0, "u", 0, 2, 8),
+    (0, "u", 0, 3, 8), (0, "u", 1, 0, 2), (1, "u", 1, 0, 0), (1, "u", 1, 1, 0), (1, "u", 1, 2, 0), (1, "u", 1, 3, 0),
+    (0, "u", 1, 1, 2), (0, "u", 1, 2, 2), (0, "u", 1, 3, 2), (1, "u", 1, 0, 1), (0, "u", 1, 0, 3), (1, "u", 1, 1, 1),
+    (1, "u", 1, 2, 1), (0, "u", 1, 1, 3), (1, "u", 1, 3, 1), (1, "u", 0, 0, 8), (1, "u", 0, 1, 8), (1, "u", 0, 2, 8),
+    (1, "u", 0, 3, 8), (0, "u", 1, 2, 3), (0, "u", 1, 3, 3), (1, "u", 1, 0, 2), (0, "u", 1, 0, 4), (1, "u", 1, 1, 2),
+    (1, "u", 1, 2, 2), (0, "u", 1, 1, 4), (1, "u", 1, 3, 2), (0, "u", 1, 2, 4), (0, "u", 1, 3, 4), (1, "u", 1, 0, 3),
+    (0, "u", 1, 0, 5), (1, "u", 1, 1, 3), (1, "u", 1, 2, 3), (0, "u", 1, 1, 5), (1, "u", 1, 3, 3), (0, "u", 1, 2, 5),
+    (0, "u", 1, 3, 5), (1, "u", 1, 0, 4), (0, "u", 1, 0, 6), (1, "u", 1, 1, 4), (1, "u", 1, 2, 4), (0, "u", 1, 1, 6),
+    (1, "u", 1, 3, 4), (0, "u", 1, 2, 6), (1, "u", 1, 0, 5), (1, "u", 1, 1, 5), (0, "u", 1, 3, 6), (1, "u", 1, 2, 5),
+    (0, "u", 1, 0, 7), (1, "u", 1, 3, 5), (0, "u", 1, 1, 7), (0, "u", 1, 2, 7), (1, "u", 1, 0, 6), (1, "u", 1, 1, 6),
+    (0, "u", 1, 3, 7), (1, "u", 1, 2, 6), (1, "u", 1, 3, 6), (1, "u", 1, 0, 7), (1, "u", 1, 1, 7), (1, "u", 1, 2, 7),
+    (1, "u", 1, 3, 7), (0, "u", 0, 0, 7), (0, "u", 0, 1, 7), (0, "u", 0, 2, 7), (0, "u", 0, 3, 7), (1, "u", 0, 0, 7),
+    (1, "u", 0, 1, 7), (1, "u", 0, 2, 7), (1, "u", 0, 3, 7),
 )
 
 
@@ -188,9 +189,11 @@
         sems.copy(own, own, sent, got, at(1)).start()
         sems.copy(own, own, sent, got, at(3)).start()
 
-    def gather_middle(buf, rows, size, at, sent, first, got):
+    def gather_arrived(buf, size, first):
+        sems.got(buf.at[pl.ds(0, 2 * size)], first)
+
+    def gather_onward(buf, rows, size, at, sent, got):
         h = size // 2
-        sems.got(buf.at[pl.ds(0, 2 * size)], first)
         left, right = buf.at[m8(rows[3], h)], buf.at[m8(rows[1] + h, h)]
         sems.copy(left, left, sent, got, at(1)).start()
         sems.copy(right, right, sent, got, at(3)).start()
@@ -473,7 +476,8 @@
                 gather_start(out, zr, UZ, at_z, zs_, slot["g1"])
 
             def gz_middle():
-                gather_middle(out, zr, UZ, at_z, zs_, slot["g1"], slot["g2"])
+                gather_arrived(out, UZ, slot["g1"])
+                gather_onward(out, zr, UZ, at_z, zs_, slot["g2"])
 
             def gx_start():
                 sems.got(out.at[pl.ds(0, UZ)], slot["g2"])
@@ -482,14 +486,19 @@
                     send_slab(u, 0)
 
             def gx_middle():
-                gather_middle(out, xr, US, at_x, gs_, slot["g3"], slot["g4"])
+                gather_arrived(out, US, slot["g3"])
                 if phase == 0:
                     send_slab(u, 1)
+                else:
+                    gx_onward()
+
+            def gx_onward():
+                gather_onward(out, xr, US, at_x, gs_, slot["g4"])
 
             def gx_end():
                 sems.got(out.at[pl.ds(0, US)], slot["g4"])
 
-            return [x_middle, x_end, z_middle, z_end, gz_middle, gx_start, gx_middle, gx_end]
+            return [x_middle, x_end, z_middle, z_end, gz_middle, gx_start, gx_middle, gx_end, gx_onward]
 
         turn = lax.rem(y - zh + 4, 4)
         root = jnp.logical_and(fetches, turn == 0)

time: 140 us -> 142 us (1.014)
  no operation moved by 1% of the time
where the time goes in v4:
time: 142 us; the launch traced here: 141 us
  Pallas kernels  140 us (99%)
    pallas_call x1, Pallas kernels, body(): pl.pallas_call(kernel, out_shape=(pltpu.VMEM((CHUNKS, ROWS, W), F32), plt...  138 us

profile of v4, /device:TPU:16, one launch (start us, length us, event | category | flops | bytes accessed | tf_op | source)
XLA Modules:
  0.0 140.9 jit_solution(3127077265015364020)
XLA Ops:
  0.6 138.2 %shard_map.30 = (f32[2,2048,128]{2,1,0:T(8,128)S(1)}, f32[2,2048,128]{2,1,0:T(8,128)S(1)}) custom-call(f32[2048,1024]{1,0:T(8,128)} %x_hbm.1), custom_call_target="tpu_custom_call" | custom-call | tf_op jit(solution)/shard_map/pallas_call | solution.py:618
  138.9 2.0 %shard_map.31 = (f32[2048,256]{1,0:T(8,128)}, f32[2048,256]{1,0:T(8,128)}) custom-call(f32[2,2048,128]{2,1,0:T(8,128)S(1)} %get-tuple-element.4.square, f32[2,2048,128]{2,1,0:T(8,128)S(1)} %get-tuple-element.5.new), custom_call_target="tpu_custom_call" | custom-call | tf_op jit(solution)/shard_map/pallas_call | solution.py:652
